TPU v7x, 128 devices: a whole 4x4x4 slice. The times are simulated.
128 devices in a mesh: seq: 16 (over x, y), head: 8 (over z, core).
Axes of the slice: x: 4, y: 4, z: 4, core: 2. Of those that a mesh axis runs over, the one named last changes fastest.
Arguments:
- attn_q: bfloat16 [16384, 5120], P('seq', 'head'), may hold values from -6 to 6
- attn_k: bfloat16 [16384, 5120], P('seq', 'head'), may hold values from -6 to 6
- attn_v: bfloat16 [16384, 5120], P('seq', 'head'), may hold values from -6 to 6
- fast_q: bfloat16 [16384, 5120], P('seq', 'head'), may hold values from -6 to 6
- fast_k: bfloat16 [16384, 5120], P('seq', 'head'), may hold values from -6 to 6
- fast_v: bfloat16 [16384, 5120], P('seq', 'head'), may hold values from -6 to 6
- rates: float32 [16384, 8], P('seq', 'head'), may hold values from 0.00015625 to 0.0015625
- fast_gate: float32 [8, 640, 640], P('head'), may hold values from -0.25 to 0.25
- fast_up: float32 [8, 640, 640], P('head'), may hold values from -0.25 to 0.25
- fast_down: float32 [8, 640, 640], P('head'), may hold values from -0.25 to 0.25
Outputs:
- mixed: bfloat16 [16384, 5120], P('seq', 'head')
All inputs are finite; a program needn't handle non-finite values.
Results may differ from a plain program's by a relative error of at most 0.012.
Values may be sent and summed in bfloat16 or wider, within the bound.
A program may use at most 128 MiB of HBM per device.

v0:
```python
import math

import jax
import jax.numpy as jnp
from jax import lax
from jax.sharding import PartitionSpec as P

HD = 128
FWD = 640
WINDOW = 1024


epsilon = 1e-06


def shifted(block, axis, distance):
    devices = range(lax.axis_size(axis))
    route = [(i - distance, i) for i in devices if i - distance in devices]
    return lax.ppermute(block, axis, route)


def sent_together(arrays, axis, dim, along):
    ends, at = ([], 0)
    for a in arrays[:-1]:
        at += a.shape[along]
        ends.append(at)
    both = jnp.concatenate(arrays, axis=along)
    return tuple(
        jnp.split(lax.psum_scatter(both, axis, scatter_dimension=dim, tiled=True), ends, axis=along)
    )


def sent_to_all(array, axis):
    copies = jnp.broadcast_to(array, (lax.axis_size(axis), *array.shape))
    return lax.all_to_all(copies, axis, split_axis=0, concat_axis=0, tiled=True)


def joined_along(pieces, dim):
    pieces = jnp.moveaxis(pieces, 0, dim)
    lengths = pieces.shape
    return pieces.reshape(*lengths[:dim], lengths[dim] * lengths[dim + 1], *lengths[dim + 2 :])


def collect(array, axis, dim):
    pieces = sent_to_all(array, axis)
    return joined_along(pieces, dim)


def side_by_side(arrays, axis, dim, along):
    both = jnp.concatenate(arrays, axis=along)
    filled, at, gathered = (collect(both, axis, dim), 0, [])
    for a in arrays:
        gathered.append(lax.slice_in_dim(filled, at, at + a.shape[along], axis=along))
        at += a.shape[along]
    return tuple(gathered)


def renorm(previous, gradient):
    updated = previous - gradient
    old_norm = jnp.sqrt(jnp.sum(previous * previous, axis=-2, keepdims=True))
    new_norm = jnp.sqrt(jnp.sum(updated * updated, axis=-2, keepdims=True) + epsilon)
    return updated * (old_norm / new_norm)


def window_attention(attn_q, attn_k, attn_v):
    rows_here = attn_q.shape[0]
    span_cols = attn_q.shape[1]
    local_heads = span_cols // HD
    first_global = lax.axis_index("seq") * rows_here
    moved_keys, moved_values = shifted((attn_k, attn_v), "seq", 1)
    key_parts = [moved_keys]
    value_parts = [moved_values]
    ext_keys = jnp.concatenate(key_parts + [attn_k], axis=0)
    ext_values = jnp.concatenate(value_parts + [attn_v], axis=0)
    block_rows = min(512, rows_here)
    inverse_root = 1.0 / math.sqrt(HD)
    results = []
    for block_index in range(rows_here // block_rows):
        first_row = block_index * block_rows
        query = attn_q[first_row : first_row + block_rows].reshape(block_rows, local_heads, HD)
        key_block = ext_keys[first_row : first_row + WINDOW + block_rows].reshape(
            WINDOW + block_rows, local_heads, HD
        )
        value_block = ext_values[first_row : first_row + WINDOW + block_rows].reshape(
            WINDOW + block_rows, local_heads, HD
        )
        scores = (
            jnp.einsum("qhd,khd->hqk", query, key_block, preferred_element_type=jnp.float32)
            * inverse_root
        )
        query_pos = first_global + first_row + jnp.arange(block_rows, dtype=jnp.int32)
        key_pos = (
            first_global + first_row - WINDOW + jnp.arange(WINDOW + block_rows, dtype=jnp.int32)
        )
        distance = query_pos[:, None] - key_pos[None, :]
        allowed = (distance >= 0) & (distance <= WINDOW) & (key_pos[None, :] >= 0)
        scores = jnp.where(allowed[None], scores, -jnp.inf)
        row_max = jnp.max(scores, axis=-1, keepdims=True)
        expo = jnp.exp(scores - row_max)
        weights = (expo / jnp.sum(expo, axis=-1, keepdims=True)).astype(jnp.bfloat16)
        result = jnp.einsum(
            "hqk,khd->qhd", weights, value_block, preferred_element_type=jnp.float32
        )
        results.append(result.reshape(block_rows, span_cols))
    return jnp.concatenate(results, axis=0)


def shards(attn_q, attn_k, attn_v, fast_q, fast_k, fast_v, rates, fast_gate, fast_up, fast_down):
    attended = window_attention(attn_q, attn_k, attn_v)
    rows_here = fast_q.shape[0]
    fast_heads = fast_gate.shape[0]
    key_rows = fast_k.reshape(rows_here, fast_heads, FWD)
    value_rows = fast_v.reshape(rows_here, fast_heads, FWD)
    query_rows = fast_q.reshape(rows_here, fast_heads, FWD)
    gate_b = fast_gate.astype(jnp.bfloat16)
    up_b = fast_up.astype(jnp.bfloat16)
    down_b = fast_down.astype(jnp.bfloat16)
    pre_gate = jnp.einsum("thd,hde->the", key_rows, gate_b, preferred_element_type=jnp.float32)
    pre_up = jnp.einsum("thd,hde->the", key_rows, up_b, preferred_element_type=jnp.float32)
    activated = jax.nn.silu(pre_gate)
    hidden = (activated * pre_up).astype(jnp.bfloat16)
    out_grad = (-rates[:, :, None] * value_rows).astype(jnp.bfloat16)
    hidden_grad = jnp.einsum("the,hfe->thf", out_grad, down_b, preferred_element_type=jnp.float32)
    sigma = jax.nn.sigmoid(pre_gate)
    gate_grad = (hidden_grad * pre_up * sigma * (1.0 + pre_gate * (1.0 - sigma))).astype(
        jnp.bfloat16
    )
    up_grad = (hidden_grad * activated).astype(jnp.bfloat16)
    grad_gate = jnp.einsum("thd,thf->hdf", key_rows, gate_grad, preferred_element_type=jnp.float32)
    grad_up = jnp.einsum("thd,thf->hdf", key_rows, up_grad, preferred_element_type=jnp.float32)
    grad_down = jnp.einsum("thf,the->hfe", hidden, out_grad, preferred_element_type=jnp.float32)
    shares = sent_together((grad_gate, grad_up, grad_down), "seq", 2, 0)
    share_cols = shares[0].shape[2]
    offset = lax.axis_index("seq") * share_cols
    part_gate = renorm(
        lax.dynamic_slice_in_dim(fast_gate, offset, share_cols, 2), shares[0]
    ).astype(jnp.bfloat16)
    part_up = renorm(lax.dynamic_slice_in_dim(fast_up, offset, share_cols, 2), shares[1]).astype(
        jnp.bfloat16
    )
    part_down = renorm(
        lax.dynamic_slice_in_dim(fast_down, offset, share_cols, 2), shares[2]
    ).astype(jnp.bfloat16)
    new_gate, new_up, new_down = side_by_side((part_gate, part_up, part_down), "seq", 2, 0)
    query_gate = jnp.einsum(
        "thd,hde->the", query_rows, new_gate, preferred_element_type=jnp.float32
    )
    query_up = jnp.einsum("thd,hde->the", query_rows, new_up, preferred_element_type=jnp.float32)
    query_hidden = (jax.nn.silu(query_gate) * query_up).astype(jnp.bfloat16)
    applied = jnp.einsum("thf,hfe->the", query_hidden, new_down, preferred_element_type=jnp.float32)
    applied = applied.reshape(rows_here, fast_heads * FWD)
    return (attended + applied).astype(jnp.bfloat16)


def solution(mesh):
    placed = (
        P("seq", "head"),
        P("seq", "head"),
        P("seq", "head"),
        P("seq", "head"),
        P("seq", "head"),
        P("seq", "head"),
        P("seq", "head"),
        P("head", None, None),
        P("head", None, None),
        P("head", None, None),
    )
    return jax.shard_map(
        shards, mesh=mesh, in_specs=placed, out_specs=P("seq", "head"), check_vma=False
    )
```

profile of v0, /device:TPU:0, one launch (start us, length us, event | category | flops | bytes accessed | tf_op | source)
XLA Modules:
  0.0 189.8 jit_solution(1826851626071821298)
XLA Ops:
  7.9 2.7 %fusion.44 = f32[640,1024]{0,1:T(8,128)S(1)} fusion(bf16[1024,640]{1,0:T(8,128)(2,1)S(1)} %copy-done, f32[1,640,640]{2,1,0:T(8,128)} %param.18), kind=kOutput, calls=%fused_computation.68 | convolution fusion | flops 839270400 | bytes 5570560 | tf_op jit(solution)/shard_map/thd,hde->the/dot_general | solution.py:119
  10.6 1.3 fusion.42
  12.4 1.4 fusion.46
  13.8 1.7 convolution_bitcast_fusion
  15.5 1.5 convolution_bitcast_fusion.1
  17.0 1.7 convolution_bitcast_fusion.2
  18.7 2.5 %pad_maximum_fusion = f32[3,640,640]{1,2,0:T(8,128)} fusion(f32[1,640,640]{1,2,0:T(8,128)S(1)} %convolution_bitcast_fusion, f32[1,640,640]{1,2,0:T(8,128)S(1)} %convolution_bitcast_fusion.1, f32[1,640,640]{1,2,0:T(8,128)S(1)} %convolution_bitcast_fusion.2), kind=kLoop, calls=%fused_computation.18 | loop fusion | flops 2457600 | bytes 9830400 | tf_op jit(solution)/shard_map/concatenate | solution.py:27
  21.2 4.8 %collective-permute-start = (bf16[1024,640]{1,0:T(8,128)(2,1)}, bf16[1024,640]{1,0:T(8,128)(2,1)}, u32[]{:S(2)}, u32[]{:S(2)}) collective-permute-start(bf16[1024,640]{1,0:T(8,128)(2,1)} %param.12), channel_id=1, source_target_pairs={{0,8},{8,16},{16,24},{24,32},{32,40},{40,48},{48,56},{56,64},{64,7... | collective-permute-start | bytes 3932168 | tf_op jit(solution)/shard_map/ppermute | solution.py:19
  26.6 3.5 %collective-permute-start.1 = (bf16[1024,640]{0,1:T(8,128)(2,1)S(1)}, bf16[1024,640]{0,1:T(8,128)(2,1)}, u32[]{:S(2)}, u32[]{:S(2)}) collective-permute-start(bf16[1024,640]{0,1:T(8,128)(2,1)S(1)} %copy.47), channel_id=1, source_target_pairs={{0,8},{8,16},{16,24},{24,32},{32,40},{40,48},{48,56},{56,64},{64,7... | collective-permute-start | bytes 3932168 | tf_op jit(solution)/shard_map/ppermute | solution.py:19
  30.1 1.4 fusion.61
  35.2 1.5 constant_dynamic-slice_fusion
  37.7 2.0 %fusion.15 = pred[512,1536]{0,1:T(8,128)(4,1)} fusion(s32[1536]{0:T(1024)S(1)} %iota_add_fusion, s32[512]{0:T(512)S(1)} %iota_add_fusion.2, pred[1536]{0:T(1024)(128)(4,1)S(1)} %broadcast_compare_fusion), kind=kLoop, calls=%fused_computation.26 | loop fusion | flops 3932160 | bytes 796160 | tf_op jit(solution)/shard_map/and | solution.py:96
  39.7 1.9 %fusion.13 = pred[512,1536]{0,1:T(8,128)(4,1)} fusion(s32[1536]{0:T(1024)S(1)} %iota_add_fusion.1, s32[512]{0:T(512)S(1)} %iota_add_fusion.3, pred[1536]{0:T(1024)(128)(4,1)S(1)} %broadcast_compare_fusion.1), kind=kLoop, calls=%fused_computation.24 | loop fusion | flops 3932160 | bytes 796160 | tf_op jit(solution)/shard_map/and | solution.py:96
  41.6 26.1 %collective-permute-done = bf16[1024,640]{1,0:T(8,128)(2,1)} collective-permute-done((bf16[1024,640]{1,0:T(8,128)(2,1)}, bf16[1024,640]{1,0:T(8,128)(2,1)}, u32[]{:S(2)}, u32[]{:S(2)}) %collective-permute-start) | collective-permute-done | bytes 1310752 | tf_op jit(solution)/shard_map/ppermute | solution.py:19
  67.7 1.4 constant_dynamic-update-slice_fusion.1
  69.1 1.6 constant_dynamic-update-slice_fusion
  70.7 1.6 fusion.59
  72.3 2.4 %copy.53 = bf16[1536,640]{0,1:T(8,128)(2,1)} copy(bf16[1536,640]{1,0:T(8,128)(2,1)S(1)} %get-tuple-element.14) | data formatting | bytes 3932160 | tf_op jit(solution)/shard_map/slice | solution.py:84
  74.8 26.2 %collective-permute-done.1 = bf16[1024,640]{0,1:T(8,128)(2,1)} collective-permute-done((bf16[1024,640]{0,1:T(8,128)(2,1)S(1)}, bf16[1024,640]{0,1:T(8,128)(2,1)}, u32[]{:S(2)}, u32[]{:S(2)}) %collective-permute-start.1) | collective-permute-done | bytes 1310752 | tf_op jit(solution)/shard_map/ppermute | solution.py:19
  101.0 3.2 %fusion.30 = (bf16[1536,640]{0,1:T(8,128)(2,1)}, bf16[1536,640]{0,1:T(8,128)(2,1)}) fusion(bf16[1024,640]{0,1:T(8,128)(2,1)} %collective-permute-done.1, bf16[1024,640]{0,1:T(8,128)(2,1)S(1)} %copy.47), kind=kLoop, calls=%fused_computation.55 | loop fusion | flops 7864320 | bytes 6553600 | tf_op jit(solution)/shard_map/concatenate | solution.py:73
  104.2 13.5 %fusion.62 = (f32[5,512]{1,0:T(8,128)S(1)}, f32[5,512,1536]{1,2,0:T(8,128)}) fusion(pred[512,1536]{0,1:T(8,128)(4,1)} %fusion.15, bf16[1536,5,128]{0,2,1:T(8,128)(2,1)} %bitcast.193, bf16[512,5,128]{0,2,1:T(8,128)(2,1)} %bitcast.199), kind=kOutput, calls=%fused_computation.113 | convolution fusion | flops 1022363136 | bytes 19146752 | tf_op jit(solution)/shard_map/sub | solution.py:99
  117.7 7.9 %fusion.11 = f32[5,128,512]{2,1,0:T(8,128)} fusion(bf16[1536,5,128]{0,2,1:T(8,128)(2,1)S(1)} %bitcast.192, f32[5,512,1536]{1,2,0:T(8,128)} %get-tuple-element.24, f32[5,512]{1,0:T(8,128)S(1)} %get-tuple-element.23), kind=kOutput, calls=%fused_computation.17 | convolution fusion | flops 1014497280 | bytes 19015680 | tf_op jit(solution)/shard_map/hqk,khd->qhd/dot_general | solution.py:101
  125.5 1.4 reduce-scatter.2.cloned.1.call-done
  129.3 1.6 broadcast_in_dim.23
  130.9 6.8 %all-to-all-start = ((bf16[16,3,640,40]{2,3,1,0:T(8,128)(2,1)}), bf16[16,3,640,40]{2,3,1,0:T(8,128)(2,1)S(1)}, u32[]{:S(2)}, u32[]{:S(2)}) async-start(bf16[16,3,640,40]{2,3,1,0:T(8,128)(2,1)} %broadcast_in_dim.23), calls=%async_computation.1 | async-start | bytes 4915200 | tf_op jit(solution)/shard_map/all_to_all | solution.py:35
  137.7 13.1 %fusion.63 = (f32[5,512]{1,0:T(8,128)S(1)}, f32[5,512,1536]{1,2,0:T(8,128)}) fusion(pred[512,1536]{0,1:T(8,128)(4,1)S(1)} %copy-done.8, bf16[1536,5,128]{0,2,1:T(8,128)(2,1)} %bitcast.191, bf16[512,5,128]{0,2,1:T(8,128)(2,1)} %bitcast.198), kind=kOutput, calls=%fused_computation.114 | convolution fusion | flops 1022363136 | bytes 19146752 | tf_op jit(solution)/shard_map/sub | solution.py:99
  150.8 4.0 %copy.46 = bf16[1536,640]{0,1:T(8,128)(2,1)} copy(bf16[1536,640]{1,0:T(8,128)(2,1)} %get-tuple-element.13) | data formatting | bytes 3932160 | tf_op jit(solution)/shard_map/slice | solution.py:84
  154.8 8.3 %fusion.10 = f32[5,128,512]{2,1,0:T(8,128)} fusion(bf16[1536,5,128]{0,2,1:T(8,128)(2,1)} %bitcast.194, f32[5,512,1536]{1,2,0:T(8,128)} %get-tuple-element.26, f32[5,512]{1,0:T(8,128)S(1)} %get-tuple-element.25), kind=kOutput, calls=%fused_computation.16 | convolution fusion | flops 1014497280 | bytes 19015680 | tf_op jit(solution)/shard_map/hqk,khd->qhd/dot_general | solution.py:101
  163.2 8.0 %all-to-all-done = bf16[16,3,640,40]{2,3,1,0:T(8,128)(2,1)S(1)} async-done(((bf16[16,3,640,40]{2,3,1,0:T(8,128)(2,1)}), bf16[16,3,640,40]{2,3,1,0:T(8,128)(2,1)S(1)}, u32[]{:S(2)}, u32[]{:S(2)}) %all-to-all-start) | async-done | bytes 2457632 | tf_op jit(solution)/shard_map/all_to_all | solution.py:35
  173.0 2.8 %fusion.64 = f32[640,1024]{0,1:T(8,128)} fusion(bf16[640,640]{0,1:T(8,128)(2,1)S(1)} %bitcast.197, bf16[1024,640]{1,0:T(8,128)(2,1)S(1)} %copy-done.10), kind=kOutput, calls=%fused_computation.115 | convolution fusion | flops 838860800 | bytes 4751360 | tf_op jit(solution)/shard_map/thd,hde->the/dot_general | solution.py:145
  175.9 5.6 %fusion.16 = bf16[1024,640]{0,1:T(8,128)(2,1)S(1)} fusion(f32[512,640]{0,1:T(8,128)} %bitcast.202, f32[512,640]{0,1:T(8,128)} %bitcast.203, bf16[640,640]{0,1:T(8,128)(2,1)} %bitcast.196, bf16[640,640]{0,1:T(8,128)(2,1)S(1)} %bitcast.195, bf16[1024,640]{1,0:T(8,128)(2,1)} %param.13, f32[640,1024]{0,1:T(8,128)} %fusion.64), kind=kOutput, calls=%fused_computation.30 | convolution fusion | flops 1683619840 | bytes 9502720 | tf_op jit(solution)/shard_map/thf,hfe->the/dot_general | solution.py:150
  181.5 1.4 copy.67
  (46 shorter events, 11.3 us)
Async XLA Ops:
  6.5 1.3 copy-start
  6.5 4.1 %copy-start.2 = (f32[1,640,640]{2,1,0:T(8,128)S(1)}, f32[1,640,640]{2,1,0:T(8,128)}, u32[]{:S(2)}) copy-start(f32[1,640,640]{2,1,0:T(8,128)} %param.17) | copy-start | bytes 4915204
  6.5 120.4 %reduce-scatter.2.cloned.1.call-start = ((), (), s32[]{:S(2)}) async-start(), calls=%async_computation.2 | async-start | bytes 5222400 | tf_op jit(solution)/shard_map/reduce_scatter | solution.py:29
  10.6 1.4 copy-start.9
  10.6 1.4 copy-start.3
  10.6 1.8 copy-start.6
  21.2 4.8 %copy-start.5 = (bf16[1024,640]{1,0:T(8,128)(2,1)S(1)}, bf16[1024,640]{1,0:T(8,128)(2,1)}, u32[]{:S(2)}) copy-start(bf16[1024,640]{1,0:T(8,128)(2,1)} %param.11) | copy-start | bytes 3932164
  21.2 46.5 %collective-permute-start = (bf16[1024,640]{1,0:T(8,128)(2,1)}, bf16[1024,640]{1,0:T(8,128)(2,1)}, u32[]{:S(2)}, u32[]{:S(2)}) collective-permute-start(bf16[1024,640]{1,0:T(8,128)(2,1)} %param.12), channel_id=1, source_target_pairs={{0,8},{8,16},{16,24},{24,32},{32,40},{40,48},{48,56},{56,64},{64,7... | collective-permute-start | bytes 3932168 | tf_op jit(solution)/shard_map/ppermute | solution.py:19
  26.6 74.3 %collective-permute-start.1 = (bf16[1024,640]{0,1:T(8,128)(2,1)S(1)}, bf16[1024,640]{0,1:T(8,128)(2,1)}, u32[]{:S(2)}, u32[]{:S(2)}) collective-permute-start(bf16[1024,640]{0,1:T(8,128)(2,1)S(1)} %copy.47), channel_id=1, source_target_pairs={{0,8},{8,16},{16,24},{24,32},{32,40},{40,48},{48,56},{56,64},{64,7... | collective-permute-start | bytes 3932168 | tf_op jit(solution)/shard_map/ppermute | solution.py:19
  104.2 13.5 %copy-start.4 = (bf16[1536,640]{0,1:T(8,128)(2,1)S(1)}, bf16[1536,640]{0,1:T(8,128)(2,1)}, u32[]{:S(2)}) copy-start(bf16[1536,640]{0,1:T(8,128)(2,1)} %copy.53) | copy-start | bytes 5898244
  117.7 9.2 %copy-start.7 = (f32[1,640,40]{1,2,0:T(8,128)S(1)}, f32[1,640,40]{1,2,0:T(8,128)}, u32[]{:S(2)}) copy-start(f32[1,640,40]{1,2,0:T(8,128)} %copy.82) | copy-start | bytes 307204
  130.9 6.8 %copy-start.8 = (pred[512,1536]{0,1:T(8,128)(4,1)S(1)}, pred[512,1536]{0,1:T(8,128)(4,1)}, u32[]{:S(2)}) copy-start(pred[512,1536]{0,1:T(8,128)(4,1)} %fusion.13) | copy-start | bytes 2359300
  130.9 40.3 %all-to-all-start = ((bf16[16,3,640,40]{2,3,1,0:T(8,128)(2,1)}), bf16[16,3,640,40]{2,3,1,0:T(8,128)(2,1)S(1)}, u32[]{:S(2)}, u32[]{:S(2)}) async-start(bf16[16,3,640,40]{2,3,1,0:T(8,128)(2,1)} %broadcast_in_dim.23), calls=%async_computation.1 | async-start | bytes 4915200 | tf_op jit(solution)/shard_map/all_to_all | solution.py:35
  171.4 1.6 copy-start.10
  175.9 7.0 %copy-start.1 = (bf16[1024,640]{1,0:T(8,128)(2,1)S(1)}, bf16[1024,640]{1,0:T(8,128)(2,1)}, u32[]{:S(2)}) copy-start(bf16[1024,640]{1,0:T(8,128)(2,1)} %param.14) | copy-start | bytes 3932164
Sparse Core Ops, SparseCore 0:
  21.3 105.5 reduce-scatter.1
where the time goes:
time: 190 us
  waiting for transfers between devices  61.7 us (32%)
  matrix products  61.4 us (32%)
  local copies, waits for them, and re-layouts  25.9 us (14%)
  starting transfers between devices  15.1 us (8%)
  between operations  13.6 us (7%)
  other arithmetic  12 us (6%)
    ppermute x2, waiting for transfers between devices, shifted(): return lax.ppermute(block, axis, route)  52.3 us
    sub x2, matrix products, window_attention(): expo = jnp.exp(scores - row_max)  26.5 us
    dot_general x2, matrix products, window_attention(): jnp.einsum('hqk,khd->qhd', weights, value_block, preferred_element_type=j...  16.2 us
    ppermute x2, starting transfers between devices, shifted(): return lax.ppermute(block, axis, route)  8.28 us
    slice x3, local copies, waits for them, and re-layouts, window_attention(): ext_values[first_row:first_row + WINDOW + block_rows]  8.11 us
    all_to_all x1, waiting for transfers between devices, sent_to_all(): return lax.all_to_all(copies, axis, split_axis=0, concat_axis=0, tiled=True)  8.01 us
    unnamed x29, local copies, waits for them, and re-layouts  7.72 us
    all_to_all x1, starting transfers between devices, sent_to_all(): return lax.all_to_all(copies, axis, split_axis=0, concat_axis=0, tiled=True)  6.81 us
  transfers between devices with their start and end apart: 4, of which 4 were waited for; matrix products, arithmetic and copies ran while one was open for 36% of the time, Pallas kernels for 0%

commit v1 on v0

v1 whole, which is shorter than its diff:
```python
import math

import jax
import jax.numpy as jnp
from jax import lax
from jax.experimental import pallas as pl
from jax.experimental.pallas import tpu as pltpu
from jax.sharding import PartitionSpec as P

HD = 128
FWD = 640
TOK = 1024
HEADS = 5
QB = 256
TB = 512
EPS = 1e-06
MESH = pl.DeviceIdType.MESH
SCALE = math.log2(math.e) / math.sqrt(HD)
NEG = -1e30
BF = jnp.bfloat16
F32 = jnp.float32

CHUNKS = ((0, 256, "x"), (256, 256, "y"), (512, 128, "x"))


class Remote:
    def __init__(self, src, dst, send_sem, recv_sem, device):
        self.parts = src, dst, send_sem, recv_sem
        self.device = device

    def copy(self):
        return pltpu.make_async_remote_copy(
            *self.parts, device_id=self.device, device_id_type=MESH
        )

    def start(self):
        self.copy().start()

    def wait_recv(self):
        self.copy().wait_recv()

    def wait_send(self):
        self.copy().wait_send()


def up16(n):
    return (n + 15) // 16 * 16


def nt(a, b):
    return lax.dot_general(a, b, (((1,), (1,)), ((), ())), preferred_element_type=F32)


def nn(a, b):
    return lax.dot_general(a, b, (((1,), (0,)), ((), ())), preferred_element_type=F32)


def kernel(
    aq, ak, av, fq, fk, fv, rt, w1, w3, w2, out,
    aq_v, ak_v, av_v, fq_v, fk_v, fv_v, rt_v, w1_v, w3_v, w2_v,
    mstack, mbf, gsum, gbf, rx0, rx1, rx2, fb0, fb1, fb2, part, share_out, share_in,
    new_out, new_in, nstack, qn, o_send, o_recv, o_own, lse_own, lse_nb, lse_send, lse_recv,
    acc, ld_sem, q_ss, q_rs, o_ss, o_rs, l_ss, l_rs, c_ss, c_rs,
):
    seq = lax.axis_index("seq")
    head = lax.axis_index("head")
    cx = seq // 4
    cy = lax.rem(seq, 4)
    rx = (rx0, rx1, rx2)
    fb = (fb0, fb1, fb2)

    def at(axis, d):
        if axis == "x":
            return (lax.rem(cx + d + 4, 4) * 4 + cy, head)
        return (cx * 4 + lax.rem(cy + d + 4, 4), head)

    def coord(axis, d=0):
        return lax.rem((cx if axis == "x" else cy) + d + 4, 4)

    before = (lax.rem(seq + 15, 16), head)
    after = (lax.rem(seq + 1, 16), head)

    loads = []
    for i, (src, dst) in enumerate(
        (
            (w1, w1_v), (w3, w3_v), (w2, w2_v), (fk, fk_v), (fv, fv_v), (rt, rt_v),
            (ak, ak_v), (av, av_v), (aq, aq_v), (fq, fq_v),
        )
    ):
        c = pltpu.make_async_copy(src, dst, ld_sem.at[i])
        c.start()
        loads.append(c)

    barrier = pltpu.get_barrier_semaphore()
    peers = [at(a, d) for a in ("x", "y") for d in (1, -1, 2)] + [before, after]
    for p in peers:
        pl.semaphore_signal(barrier, inc=1, device_id=p, device_id_type=MESH)
    pl.semaphore_wait(barrier, len(peers))

    def lanes(h):
        if isinstance(h, int):
            return pl.ds(h * HD, HD)
        return pl.ds(pl.multiple_of(h * HD, HD), HD)

    def q_copy(h):
        return Remote(aq.at[:, lanes(h)], qn.at[h], q_ss.at[h], q_rs.at[h], before)

    def o_copy(h):
        return Remote(o_send.at[h], o_recv.at[h], o_ss.at[h], o_rs.at[h], after)

    def lse_copy():
        return Remote(lse_send, lse_recv, l_ss.at[0], l_rs.at[0], after)

    for h in range(HEADS):
        q_copy(h).start()

    def sizes(c):
        first, width, axis = CHUNKS[c]
        rows = 3 * width
        return 3 * first, width, rows, rows // 4, rows // 8, rows // 16, axis, "y" if axis == "x" else "x"

    def rows_of(base, index, n):
        return pl.ds(pl.multiple_of(base + index * n, 8 if n % 16 else 16), n)

    def rs1_copies(c):
        base, _, _, p, hf, _, a, _ = sizes(c)
        up, dn, op = coord(a, 1), coord(a, -1), coord(a, 2)
        ss, rs, r = c_ss.at[c], c_rs.at[c], rx[c]
        return (
            Remote(gbf.at[rows_of(base, op * 2, hf)], r.at[0], ss.at[0], rs.at[0], at(a, 1)),
            Remote(gbf.at[rows_of(base, op * 2 + 1, hf)], r.at[1], ss.at[1], rs.at[1], at(a, -1)),
            Remote(gbf.at[rows_of(base, up * 2 + 1, hf)], r.at[2], ss.at[2], rs.at[2], at(a, 1)),
            Remote(gbf.at[rows_of(base, dn * 2, hf)], r.at[3], ss.at[3], rs.at[3], at(a, -1)),
            Remote(fb[c].at[0], r.at[4], ss.at[4], rs.at[4], at(a, 1)),
            Remote(fb[c].at[1], r.at[5], ss.at[5], rs.at[5], at(a, -1)),
        )

    def rs1_start(c):
        for cp in rs1_copies(c)[:4]:
            cp.start()

    def rs1_mid(c):
        base, _, _, _, hf, _, a, _ = sizes(c)
        cps = rs1_copies(c)
        cps[0].wait_recv()
        fb[c][0] = (gsum[rows_of(base, coord(a, 1) * 2, hf), :] + rx[c][0].astype(F32)).astype(BF)
        cps[4].start()
        cps[1].wait_recv()
        fb[c][1] = (gsum[rows_of(base, coord(a, -1) * 2 + 1, hf), :] + rx[c][1].astype(F32)).astype(BF)
        cps[5].start()

    def rs2_copies(c):
        _, _, _, _, _, s, _, b = sizes(c)
        s = up16(s)
        ss, rs = c_ss.at[c], c_rs.at[c]
        return [
            Remote(
                share_out.at[c, d - 1, pl.ds(0, s)], share_in.at[c, d - 1, pl.ds(0, s)],
                ss.at[5 + d], rs.at[5 + d], at(b, d),
            )
            for d in (1, 2, 3)
        ]

    def rs1_end(c):
        base, _, _, p, hf, s, a, b = sizes(c)
        cps = rs1_copies(c)
        for i in (2, 3, 4, 5):
            cps[i].wait_recv()
        r = rx[c]
        mine = coord(a)
        part[pl.ds(0, hf), :] = (
            gsum[rows_of(base, mine * 2, hf), :] + r[3].astype(F32) + r[4].astype(F32)
        )
        part[pl.ds(hf, hf), :] = (
            gsum[rows_of(base, mine * 2 + 1, hf), :] + r[2].astype(F32) + r[5].astype(F32)
        )
        for d, cp in zip((1, 2, 3), rs2_copies(c)):
            share_out[c, d - 1, pl.ds(0, s), :] = part[rows_of(0, coord(b, d), s), :].astype(BF)
            cp.start()
        gsum[pl.ds(base, s), :] = part[rows_of(0, coord(b), s), :]

    def ag2_copies(c):
        _, _, _, _, _, s, _, b = sizes(c)
        s = up16(s)
        ss, rs = c_ss.at[c], c_rs.at[c]
        return [
            Remote(
                new_out.at[c, pl.ds(0, s)], new_in.at[c, d - 1, pl.ds(0, s)],
                ss.at[8 + d], rs.at[8 + d], at(b, d),
            )
            for d in (1, 2, 3)
        ]

    def rs2_end(c):
        base, width, _, p, _, s, a, b = sizes(c)
        for cp in rs2_copies(c):
            cp.wait_recv()
        total = gsum[pl.ds(base, s), :]
        for d in range(3):
            total = total + share_in[c, d, pl.ds(0, s), :].astype(F32)
        start = coord(a) * p + coord(b) * s
        old = mstack[pl.ds(pl.multiple_of(base + start, 8), s), :]
        new = old - total
        old_norm = jnp.sqrt(jnp.sum(old * old, axis=1, keepdims=True))
        new_norm = jnp.sqrt(jnp.sum(new * new, axis=1, keepdims=True) + EPS)
        row = start + lax.broadcasted_iota(jnp.int32, (s, 1), 0)
        factor = jnp.where(row < 2 * width, old_norm / new_norm, 1.0)
        new_out[c, pl.ds(0, s), :] = (new * factor).astype(BF)
        for cp in ag2_copies(c):
            cp.start()

    def ag1_copies(c):
        base, _, _, p, hf, _, a, _ = sizes(c)
        ss, rs = c_ss.at[c], c_rs.at[c]
        me, dn, up = coord(a), coord(a, -1), coord(a, 1)

        def same(rows, i, d):
            return Remote(nstack.at[rows], nstack.at[rows], ss.at[i], rs.at[i], at(a, d))

        return (
            same(rows_of(base, me, p), 12, 1),
            same(rows_of(base, me, p), 13, -1),
            same(rows_of(base, dn * 2, hf), 14, 1),
            same(rows_of(base, up * 2 + 1, hf), 15, -1),
        )

    def ag2_end(c):
        base, _, _, p, _, s, a, b = sizes(c)
        for cp in ag2_copies(c):
            cp.wait_recv()
        part[rows_of(0, coord(b), s), :] = new_out[c, pl.ds(0, s), :].astype(F32)
        for d in (1, 2, 3):
            part[rows_of(0, coord(b, -d), s), :] = new_in[c, d - 1, pl.ds(0, s), :].astype(F32)
        nstack[rows_of(base, coord(a), p), :] = part[pl.ds(0, p), :].astype(BF)
        cps = ag1_copies(c)
        cps[0].start()
        cps[1].start()

    def ag1_fwd(c):
        cps = ag1_copies(c)
        cps[0].wait_recv()
        cps[2].start()
        cps[1].wait_recv()
        cps[3].start()

    def ag1_end(c):
        cps = ag1_copies(c)
        cps[2].wait_recv()
        cps[3].wait_recv()

    def prepare(c):
        first, width, _ = CHUNKS[c]
        base = 3 * first
        for k in range(width // 128):
            cols = pl.ds(first + k * 128, 128)
            for n, ref in ((0, w1_v), (1, w3_v)):
                t = ref[:, cols].T
                mstack[pl.ds(base + n * width + k * 128, 128), :] = t
                mbf[pl.ds(base + n * width + k * 128, 128), :] = t.astype(BF)
        t = w2_v[pl.ds(first, width), :]
        mstack[pl.ds(base + 2 * width, width), :] = t
        mbf[pl.ds(base + 2 * width, width), :] = t.astype(BF)

    def grads(c):
        first, width, _ = CHUNKS[c]
        base = 3 * first
        rows = [pl.ds(base + n * width, width) for n in range(3)]

        def tokens(i, _):
            tok = pl.ds(pl.multiple_of(i * TB, TB), TB)
            key = fk_v[tok, :]
            og = fv_v[tok, :]
            pg = nt(mbf[rows[0], :], key)
            pu = nt(mbf[rows[1], :], key)
            hg = nt(mbf[rows[2], :], og)
            sg = jax.nn.sigmoid(pg)
            act = pg * sg
            hidden = (act * pu).astype(BF)
            gg = (hg * pu * sg * (1.0 + pg * (1.0 - sg))).astype(BF)
            ug = (hg * act).astype(BF)
            for r, lhs, rhs in ((rows[0], gg, key), (rows[1], ug, key), (rows[2], hidden, og)):
                gsum[r, :] += nn(lhs, rhs)
            return 0

        for r in rows:
            gsum[r, :] = jnp.zeros((width, FWD), F32)
        lax.fori_loop(0, TOK // TB, tokens, 0)
        whole = pl.ds(base, 3 * width)
        gbf[whole, :] = gsum[whole, :].astype(BF)

    for c in loads[:6]:
        c.wait()
    for i in range(TOK // QB):
        tok = pl.ds(i * QB, QB)
        fv_v[tok, :] = (-rt_v[tok, :] * fv_v[tok, :].astype(F32)).astype(BF)
    for c in range(len(CHUNKS)):
        prepare(c)
        grads(c)
        rs1_start(c)
        if c:
            rs1_mid(c - 1)

    for c in loads[6:]:
        c.wait()
    row_i = lax.broadcasted_iota(jnp.int32, (QB, QB), 0)
    col_i = lax.broadcasted_iota(jnp.int32, (QB, QB), 1)
    lane_i = lax.broadcasted_iota(jnp.int32, (QB, HD), 1)

    def attend(q, h, i, own, lse_ref):
        diag = pl.ds(i * QB, QB)
        if own:
            lo, n = 0, i * QB
        else:
            lo, n = (i + 1) * QB, TOK - (i + 1) * QB
        sd = nt(q, ak_v[diag, lanes(h)])
        sd = jnp.where((col_i <= row_i) if own else (col_i >= row_i), sd, NEG)
        m = jnp.max(sd, axis=1, keepdims=True)
        if n:
            so = nt(q, ak_v[pl.ds(lo, n), lanes(h)])
            m = jnp.maximum(m, jnp.max(so, axis=1, keepdims=True))
        pd = jnp.exp2((sd - m) * SCALE)
        l = jnp.sum(pd, axis=1, keepdims=True)
        o = nn(pd.astype(BF), av_v[diag, lanes(h)])
        if n:
            po = jnp.exp2((so - m) * SCALE)
            l = l + jnp.sum(po, axis=1, keepdims=True)
            o = o + nn(po.astype(BF), av_v[pl.ds(lo, n), lanes(h)])
        lse = m * SCALE + jnp.log2(l)
        lse_ref[diag, :] = jnp.where(lane_i == h, lse, lse_ref[diag, :])
        return o / l

    def own(h):
        for i in range(TOK // QB):
            tok = pl.ds(i * QB, QB)
            o_own[tok, lanes(h)] = attend(aq_v[tok, lanes(h)], h, i, True, lse_own).astype(BF)

    def serve(h):
        q_copy(h).wait_recv()
        for i in range(TOK // QB):
            tok = pl.ds(i * QB, QB)
            o_send[h, tok, :] = attend(qn[h, tok, :], h, i, False, lse_nb).astype(BF)
        o_copy(h).start()

    lse_own[...] = jnp.zeros_like(lse_own)
    lse_nb[...] = jnp.zeros_like(lse_nb)

    def when(h, k, *stages):
        @pl.when(h == k)
        def _():
            for f, c in stages:
                f(c)

    def one_head(h, _):
        own(h)
        when(h, 0, (rs1_mid, 2))
        when(h, 1, (rs1_end, 1))
        when(h, 2, (rs2_end, 1))
        when(h, 3, (ag2_end, 1))
        when(h, 4, (ag2_end, 2), (ag1_fwd, 0))
        serve(h)
        when(h, 0, (rs1_end, 0))
        when(h, 1, (rs2_end, 0), (rs1_end, 2))
        when(h, 2, (ag2_end, 0), (rs2_end, 2))
        return 0

    lax.fori_loop(0, HEADS, one_head, 0)
    ag1_fwd(1)
    for i in range(TOK // HD):
        lse_send[:, pl.ds(i * HD, HD)] = lse_nb[pl.ds(i * HD, HD), :].T[0:8, :]
    lse_copy().start()
    ag1_fwd(2)

    def apply(c, first):
        base, width, *_ = sizes(c)

        def tokens(i, _):
            tok = pl.ds(pl.multiple_of(i * QB, QB), QB)
            q = fq_v[tok, :]
            pg = nt(q, nstack[pl.ds(base, width), :])
            pu = nt(q, nstack[pl.ds(base + width, width), :])
            hid = (pg * jax.nn.sigmoid(pg) * pu).astype(BF)
            o = nn(hid, nstack[pl.ds(base + 2 * width, width), :])
            if first:
                acc[tok, :] = o
            else:
                acc[tok, :] += o
            return 0

        lax.fori_loop(0, TOK // QB, tokens, 0)

    new_sq = jnp.zeros((1, FWD), F32)
    for c in range(len(CHUNKS)):
        ag1_end(c)
        apply(c, c == 0)
        base, width, *_ = sizes(c)
        u = nstack[pl.ds(base + 2 * width, width), :].astype(F32)
        new_sq = new_sq + jnp.sum(u * u, axis=0, keepdims=True)
    old = w2_v[...]
    factor = jnp.sqrt(jnp.sum(old * old, axis=0, keepdims=True)) / jnp.sqrt(new_sq + EPS)

    for h in range(HEADS):
        o_copy(h).wait_recv()
    lse_copy().wait_recv()
    for i in range(TOK // HD):
        tok = pl.ds(i * HD, HD)
        theirs = jnp.concatenate([lse_recv[:, tok], jnp.zeros((HD - 8, HD), F32)], axis=0).T
        theirs = jnp.where(seq == 0, NEG, theirs)
        keep = 1.0 / (1.0 + jnp.exp2(theirs - lse_own[tok, :]))
        for h in range(HEADS):
            k = keep[:, h : h + 1]
            o = o_own[tok, lanes(h)].astype(F32) * k + o_recv[h, tok, :].astype(F32) * (1.0 - k)
            out[tok, lanes(h)] = (o + acc[tok, lanes(h)] * factor[:, h * HD : (h + 1) * HD]).astype(BF)

    for h in range(HEADS):
        q_copy(h).wait_send()
        o_copy(h).wait_send()
    lse_copy().wait_send()
    for c in range(len(CHUNKS)):
        for cp in (*rs1_copies(c), *rs2_copies(c), *ag2_copies(c), *ag1_copies(c)):
            cp.wait_send()


def shards(attn_q, attn_k, attn_v, fast_q, fast_k, fast_v, rates, fast_gate, fast_up, fast_down):
    rows = TOK
    act = pltpu.VMEM((rows, FWD), BF)
    weight = pltpu.VMEM((FWD, FWD), F32)
    n = len(CHUNKS)
    half = [3 * w // 8 for _, w, _ in CHUNKS]
    share = max(up16(3 * w // 16) for _, w, _ in CHUNKS)
    scratch = [
        act, act, act, act, act, act, pltpu.VMEM((rows, 1), F32), weight, weight, weight,
        pltpu.VMEM((3 * FWD, FWD), F32),
        pltpu.VMEM((3 * FWD, FWD), BF),
        pltpu.VMEM((3 * FWD, FWD), F32),
        pltpu.VMEM((3 * FWD, FWD), BF),
        *[pltpu.VMEM((6, h, FWD), BF) for h in half],
        *[pltpu.VMEM((2, h, FWD), BF) for h in half],
        pltpu.VMEM((2 * max(half), FWD), F32),
        pltpu.VMEM((n, 3, share, FWD), BF),
        pltpu.VMEM((n, 3, share, FWD), BF),
        pltpu.VMEM((n, share, FWD), BF),
        pltpu.VMEM((n, 3, share, FWD), BF),
        pltpu.VMEM((3 * FWD, FWD), BF),
        pltpu.VMEM((HEADS, rows, HD), BF),
        pltpu.VMEM((HEADS, rows, HD), BF),
        pltpu.VMEM((HEADS, rows, HD), BF),
        act,
        pltpu.VMEM((rows, HD), F32),
        pltpu.VMEM((rows, HD), F32),
        pltpu.VMEM((8, rows), F32),
        pltpu.VMEM((8, rows), F32),
        pltpu.VMEM((rows, FWD), F32),
        pltpu.SemaphoreType.DMA((10,)),
        pltpu.SemaphoreType.DMA((HEADS,)),
        pltpu.SemaphoreType.DMA((HEADS,)),
        pltpu.SemaphoreType.DMA((HEADS,)),
        pltpu.SemaphoreType.DMA((HEADS,)),
        pltpu.SemaphoreType.DMA((1,)),
        pltpu.SemaphoreType.DMA((1,)),
        pltpu.SemaphoreType.DMA((n, 16)),
        pltpu.SemaphoreType.DMA((n, 16)),
    ]
    square = fast_gate.reshape(FWD, FWD), fast_up.reshape(FWD, FWD), fast_down.reshape(FWD, FWD)
    return pl.pallas_call(
        kernel,
        out_shape=jax.ShapeDtypeStruct((rows, FWD), BF),
        in_specs=[pl.BlockSpec(memory_space=pl.ANY)] * 10,
        out_specs=pl.BlockSpec(memory_space=pltpu.VMEM),
        scratch_shapes=scratch,
        compiler_params=pltpu.CompilerParams(
            collective_id=0, has_side_effects=True, vmem_limit_bytes=60 << 20
        ),
    )(attn_q, attn_k, attn_v, fast_q, fast_k, fast_v, rates, *square)


def solution(mesh):
    placed = (P("seq", "head"),) * 7 + (P("head", None, None),) * 3
    return jax.shard_map(
        shards, mesh=mesh, in_specs=placed, out_specs=P("seq", "head"), check_vma=False
    )
```

time: 190 us -> 104 us (0.55)
  the two profiles are of different devices: /device:TPU:0 before, /device:TPU:72 now
where the time goes in v1:
time: 104 us
  Pallas kernels  100 us (96%)
  local copies, waits for them, and re-layouts  4.19 us (4%)
    pallas_call x1, Pallas kernels, shards(): pl.pallas_call(kernel, out_shape=jax.ShapeDtypeStruct((rows, FWD), BF), i...  100 us
    unnamed x2, local copies, waits for them, and re-layouts  4.19 us

profile of v1, /device:TPU:72, one launch (start us, length us, event | category | flops | bytes accessed | tf_op | source)
XLA Modules:
  0.0 104.2 jit_solution(13055271927367271478)
XLA Ops:
  0.0 1.7 %copy.11.rt = f32[1024,1]{1,0:T(8,128)} copy(f32[1024,1]{0,1:T(1,128)} %param.16) | data formatting | bytes 8192 | tf_op args[6]
  1.7 100.0 %shard_map.100 = bf16[1024,640]{1,0:T(8,128)(2,1)} custom-call(bf16[1024,640]{1,0:T(8,128)(2,1)} %aq.1, bf16[1024,640]{1,0:T(8,128)(2,1)} %ak.1, bf16[1024,640]{1,0:T(8,128)(2,1)} %av.1, bf16[1024,640]{1,0:T(8,128)(2,1)} %fq.1, bf16[1024,640]{1,0:T(8,128)(2,1)} %fk.1, bf16[1024,640]{1,0:T(8,128)(2,1)} %fv.1, f32[1024,1]{1,0:T(8,128)} %copy.11.rt, ...), custom_call_target="tpu_custom_call" | custom-call | tf_op jit(solution)/shard_map/pallas_call | solution.py:464
  101.7 2.5 %copy.13 = bf16[1024,640]{1,0:T(8,128)(2,1)} copy(bf16[1024,640]{1,0:T(8,128)(2,1)} %shard_map.100) | data formatting | bytes 2621440

commit v2 on v1

--- a/solution.py
+++ b/solution.py
@@ -43,6 +43,17 @@
         self.copy().wait_send()
 
 
+ORDER = (
+    "q31", "v40", "q30", "G2", "q11", "v41", "o40", "q21", "G1", "G0", "s11", "o00",
+    "m2", "o20", "q20", "q01", "s40", "o30", "o01", "s31", "m0", "m1", "o21", "s30",
+    "e2", "o11", "s41", "e1", "e0", "s01", "q00", "r2", "r1", "r0", "s20", "q10",
+    "a2", "a1", "o10", "o31", "a0", "f2", "f1", "f0", "s21", "o41", "s10", "s00",
+    "P1", "P0", "M", "P2",
+)
+KV_HEADS = 1
+SERVED = HEADS - KV_HEADS
+
+
 def up16(n):
     return (n + 15) // 16 * 16
 
@@ -59,8 +70,8 @@
     aq, ak, av, fq, fk, fv, rt, w1, w3, w2, out,
     aq_v, ak_v, av_v, fq_v, fk_v, fv_v, rt_v, w1_v, w3_v, w2_v,
     mstack, mbf, gsum, gbf, rx0, rx1, rx2, fb0, fb1, fb2, part, share_out, share_in,
-    new_out, new_in, nstack, qn, o_send, o_recv, o_own, lse_own, lse_nb, lse_send, lse_recv,
-    acc, ld_sem, q_ss, q_rs, o_ss, o_rs, l_ss, l_rs, c_ss, c_rs,
+    new_out, new_in, nstack, qn, kn, vn, o_send, o_recv, o_own, lse_own, lse_nb, lse_kv, lse_send, lse_recv,
+    acc, ld_sem, q_ss, q_rs, o_ss, o_rs, k_ss, k_rs, l_ss, l_rs, c_ss, c_rs,
 ):
     seq = lax.axis_index("seq")
     head = lax.axis_index("head")
@@ -102,17 +113,31 @@
             return pl.ds(h * HD, HD)
         return pl.ds(pl.multiple_of(h * HD, HD), HD)
 
-    def q_copy(h):
-        return Remote(aq.at[:, lanes(h)], qn.at[h], q_ss.at[h], q_rs.at[h], before)
-
-    def o_copy(h):
-        return Remote(o_send.at[h], o_recv.at[h], o_ss.at[h], o_rs.at[h], after)
+    def half(b):
+        return pl.ds(b * TOK // 2, TOK // 2)
+
+    def q_copy(h, b):
+        return Remote(
+            aq.at[half(b), lanes(h)], qn.at[h, half(b)], q_ss.at[h, b], q_rs.at[h, b], before
+        )
+
+    def o_copy(h, b):
+        return Remote(
+            o_send.at[h, half(b)], o_recv.at[h, half(b)], o_ss.at[h, b], o_rs.at[h, b], after
+        )
+
+    def kv_copies(h, b):
+        n = h - SERVED
+        return [
+            Remote(
+                src.at[half(b), lanes(h)], dst.at[n, half(b)],
+                k_ss.at[n, b, i], k_rs.at[n, b, i], after,
+            )
+            for i, (src, dst) in enumerate(((ak, kn), (av, vn)))
+        ]
 
     def lse_copy():
         return Remote(lse_send, lse_recv, l_ss.at[0], l_rs.at[0], after)
-
-    for h in range(HEADS):
-        q_copy(h).start()
 
     def sizes(c):
         first, width, axis = CHUNKS[c]
@@ -218,8 +243,10 @@
             return Remote(nstack.at[rows], nstack.at[rows], ss.at[i], rs.at[i], at(a, d))
 
         return (
-            same(rows_of(base, me, p), 12, 1),
-            same(rows_of(base, me, p), 13, -1),
+            same(rows_of(base, me * 2, hf), 12, 1),
+            same(rows_of(base, me * 2 + 1, hf), 13, -1),
+            same(rows_of(base, me * 2 + 1, hf), 16, 1),
+            same(rows_of(base, me * 2, hf), 17, -1),
             same(rows_of(base, dn * 2, hf), 14, 1),
             same(rows_of(base, up * 2 + 1, hf), 15, -1),
         )
@@ -232,21 +259,20 @@
         for d in (1, 2, 3):
             part[rows_of(0, coord(b, -d), s), :] = new_in[c, d - 1, pl.ds(0, s), :].astype(F32)
         nstack[rows_of(base, coord(a), p), :] = part[pl.ds(0, p), :].astype(BF)
-        cps = ag1_copies(c)
-        cps[0].start()
-        cps[1].start()
+        for cp in ag1_copies(c)[:4]:
+            cp.start()
 
     def ag1_fwd(c):
         cps = ag1_copies(c)
         cps[0].wait_recv()
-        cps[2].start()
+        cps[4].start()
         cps[1].wait_recv()
-        cps[3].start()
+        cps[5].start()
 
     def ag1_end(c):
         cps = ag1_copies(c)
-        cps[2].wait_recv()
-        cps[3].wait_recv()
+        for cp in cps[2:]:
+            cp.wait_recv()
 
     def prepare(c):
         first, width, _ = CHUNKS[c]
@@ -269,16 +295,17 @@
         def tokens(i, _):
             tok = pl.ds(pl.multiple_of(i * TB, TB), TB)
             key = fk_v[tok, :]
-            og = fv_v[tok, :]
+            val = fv_v[tok, :]
+            rate = -rt_v[:, tok]
             pg = nt(mbf[rows[0], :], key)
             pu = nt(mbf[rows[1], :], key)
-            hg = nt(mbf[rows[2], :], og)
+            hg = nt(mbf[rows[2], :], val) * rate
             sg = jax.nn.sigmoid(pg)
             act = pg * sg
-            hidden = (act * pu).astype(BF)
+            hidden = (act * pu * rate).astype(BF)
             gg = (hg * pu * sg * (1.0 + pg * (1.0 - sg))).astype(BF)
             ug = (hg * act).astype(BF)
-            for r, lhs, rhs in ((rows[0], gg, key), (rows[1], ug, key), (rows[2], hidden, og)):
+            for r, lhs, rhs in ((rows[0], gg, key), (rows[1], ug, key), (rows[2], hidden, val)):
                 gsum[r, :] += nn(lhs, rhs)
             return 0
 
@@ -288,90 +315,97 @@
         whole = pl.ds(base, 3 * width)
         gbf[whole, :] = gsum[whole, :].astype(BF)
 
-    for c in loads[:6]:
-        c.wait()
-    for i in range(TOK // QB):
-        tok = pl.ds(i * QB, QB)
-        fv_v[tok, :] = (-rt_v[tok, :] * fv_v[tok, :].astype(F32)).astype(BF)
-    for c in range(len(CHUNKS)):
-        prepare(c)
-        grads(c)
-        rs1_start(c)
-        if c:
-            rs1_mid(c - 1)
-
-    for c in loads[6:]:
-        c.wait()
     row_i = lax.broadcasted_iota(jnp.int32, (QB, QB), 0)
     col_i = lax.broadcasted_iota(jnp.int32, (QB, QB), 1)
-    lane_i = lax.broadcasted_iota(jnp.int32, (QB, HD), 1)
-
-    def attend(q, h, i, own, lse_ref):
+
+    def attend(q, keys, vals, i, own, lse_ref, h):
         diag = pl.ds(i * QB, QB)
         if own:
             lo, n = 0, i * QB
         else:
             lo, n = (i + 1) * QB, TOK - (i + 1) * QB
-        sd = nt(q, ak_v[diag, lanes(h)])
+        sd = nt(q, keys(diag))
         sd = jnp.where((col_i <= row_i) if own else (col_i >= row_i), sd, NEG)
         m = jnp.max(sd, axis=1, keepdims=True)
         if n:
-            so = nt(q, ak_v[pl.ds(lo, n), lanes(h)])
+            so = nt(q, keys(pl.ds(lo, n)))
             m = jnp.maximum(m, jnp.max(so, axis=1, keepdims=True))
         pd = jnp.exp2((sd - m) * SCALE)
         l = jnp.sum(pd, axis=1, keepdims=True)
-        o = nn(pd.astype(BF), av_v[diag, lanes(h)])
+        o = nn(pd.astype(BF), vals(diag))
         if n:
             po = jnp.exp2((so - m) * SCALE)
             l = l + jnp.sum(po, axis=1, keepdims=True)
-            o = o + nn(po.astype(BF), av_v[pl.ds(lo, n), lanes(h)])
+            o = o + nn(po.astype(BF), vals(pl.ds(lo, n)))
         lse = m * SCALE + jnp.log2(l)
-        lse_ref[diag, :] = jnp.where(lane_i == h, lse, lse_ref[diag, :])
+        lse_ref[diag, pl.ds(h, 1)] = lse
         return o / l
 
-    def own(h):
-        for i in range(TOK // QB):
+    def blocks(b):
+        return range(b * TOK // QB // 2, (b + 1) * TOK // QB // 2)
+
+    def own(h, b):
+        for i in blocks(b):
             tok = pl.ds(i * QB, QB)
-            o_own[tok, lanes(h)] = attend(aq_v[tok, lanes(h)], h, i, True, lse_own).astype(BF)
-
-    def serve(h):
-        q_copy(h).wait_recv()
-        for i in range(TOK // QB):
-            tok = pl.ds(i * QB, QB)
-            o_send[h, tok, :] = attend(qn[h, tok, :], h, i, False, lse_nb).astype(BF)
-        o_copy(h).start()
+            o_own[tok, lanes(h)] = attend(
+                aq_v[tok, lanes(h)], lambda r: ak_v[r, lanes(h)], lambda r: av_v[r, lanes(h)],
+                i, True, lse_own, h,
+            )
+
+    def serve(h, b):
+        if h < SERVED:
+            q_copy(h, b).wait_recv()
+            for i in blocks(b):
+                tok = pl.ds(i * QB, QB)
+                o_send[h, tok, :] = attend(
+                    qn[h, tok, :], lambda r: ak_v[r, lanes(h)], lambda r: av_v[r, lanes(h)],
+                    i, False, lse_nb, h,
+                ).astype(BF)
+            o_copy(h, b).start()
+        else:
+            n = h - SERVED
+            for i in blocks(b):
+                tok = pl.ds(i * QB, QB)
+                o_recv[h, tok, :] = attend(
+                    aq_v[tok, lanes(h)], lambda r: kn[n, r, :], lambda r: vn[n, r, :],
+                    i, False, lse_kv, h,
+                ).astype(BF)
 
     lse_own[...] = jnp.zeros_like(lse_own)
     lse_nb[...] = jnp.zeros_like(lse_nb)
 
-    def when(h, k, *stages):
-        @pl.when(h == k)
-        def _():
-            for f, c in stages:
-                f(c)
-
-    def one_head(h, _):
-        own(h)
-        when(h, 0, (rs1_mid, 2))
-        when(h, 1, (rs1_end, 1))
-        when(h, 2, (rs2_end, 1))
-        when(h, 3, (ag2_end, 1))
-        when(h, 4, (ag2_end, 2), (ag1_fwd, 0))
-        serve(h)
-        when(h, 0, (rs1_end, 0))
-        when(h, 1, (rs2_end, 0), (rs1_end, 2))
-        when(h, 2, (ag2_end, 0), (rs2_end, 2))
-        return 0
-
-    lax.fori_loop(0, HEADS, one_head, 0)
-    ag1_fwd(1)
-    for i in range(TOK // HD):
-        lse_send[:, pl.ds(i * HD, HD)] = lse_nb[pl.ds(i * HD, HD), :].T[0:8, :]
-    lse_copy().start()
-    ag1_fwd(2)
-
-    def apply(c, first):
+    def send_lse():
+        for i in range(TOK // HD):
+            lse_send[:, pl.ds(i * HD, HD)] = lse_nb[pl.ds(i * HD, HD), :].T[0:8, :]
+        lse_copy().start()
+
+    def merge():
+        for h in range(SERVED):
+            for b in range(2):
+                o_copy(h, b).wait_recv()
+        lse_copy().wait_recv()
+        for i in range(TOK // HD):
+            tok = pl.ds(i * HD, HD)
+            theirs = jnp.concatenate([lse_recv[:, tok], jnp.zeros((HD - 8, HD), F32)], axis=0).T
+            for h in range(HEADS):
+                t = theirs[:, h : h + 1] if h < SERVED else lse_kv[tok, h : h + 1]
+                t = jnp.where(seq == 0, NEG, t)
+                k = 1.0 / (1.0 + jnp.exp2(t - lse_own[tok, h : h + 1]))
+                o_own[tok, lanes(h)] = (
+                    o_own[tok, lanes(h)] * k + o_recv[h, tok, :].astype(F32) * (1.0 - k)
+                )
+
+    squares = []
+
+    def apply(c, first, last):
         base, width, *_ = sizes(c)
+        u = nstack[pl.ds(base + 2 * width, width), :].astype(F32)
+        squares.append(jnp.sum(u * u, axis=0, keepdims=True))
+        if last:
+            old = w2_v[...]
+            factor = jnp.sqrt(jnp.sum(old * old, axis=0, keepdims=True)) / jnp.sqrt(
+                sum(squares) + EPS
+            )
 
         def tokens(i, _):
             tok = pl.ds(pl.multiple_of(i * QB, QB), QB)
@@ -380,40 +414,82 @@
             pu = nt(q, nstack[pl.ds(base + width, width), :])
             hid = (pg * jax.nn.sigmoid(pg) * pu).astype(BF)
             o = nn(hid, nstack[pl.ds(base + 2 * width, width), :])
-            if first:
+            if not first:
+                o = acc[tok, :] + o
+            if last:
+                out[tok, :] = (o_own[tok, :] + o * factor).astype(BF)
+            else:
                 acc[tok, :] = o
+            return 0
+
+        lax.fori_loop(0, TOK // QB, tokens, 0)
+
+    waited = set()
+
+    def loaded(*names):
+        for i in names:
+            if i not in waited:
+                waited.add(i)
+                loads[i].wait()
+
+    applied = [0]
+    merged = [False]
+    left = set((h, b) for h in range(SERVED) for b in range(2))
+    for token in ORDER:
+        kind, first = token[0], int(token[1:2] or 0)
+        b = int(token[2]) if len(token) > 2 else 0
+        if kind == "q":
+            q_copy(first, b).start()
+        elif kind == "v":
+            for cp in kv_copies(first, b):
+                cp.start()
+        elif kind == "o":
+            loaded(6, 7, 8)
+            own(first, b)
+        elif kind == "s":
+            loaded(6, 7, 8)
+            if first >= SERVED:
+                for part_ in (1, 0):
+                    if part_ >= b and (first, part_) not in waited:
+                        waited.add((first, part_))
+                        for cp in kv_copies(first, part_):
+                            cp.wait_recv()
+            serve(first, b)
+            if first < SERVED:
+                left.discard((first, b))
+                if not left:
+                    send_lse()
+        elif kind == "G":
+            loaded(*range(6))
+            prepare(first)
+            grads(first)
+            rs1_start(first)
+        elif kind == "m":
+            rs1_mid(first)
+        elif kind == "e":
+            rs1_end(first)
+        elif kind == "r":
+            rs2_end(first)
+        elif kind == "a":
+            ag2_end(first)
+        elif kind == "f":
+            ag1_fwd(first)
+        elif kind == "M":
+            merge()
+        elif kind == "P":
+            loaded(9)
+            ag1_end(first)
+            applied[0] += 1
+            apply(first, applied[0] == 1, applied[0] == len(CHUNKS))
+
+    for h in range(HEADS):
+        for b in range(2):
+            if h < SERVED:
+                q_copy(h, b).wait_send()
+                o_copy(h, b).wait_send()
             else:
-                acc[tok, :] += o
-            return 0
-
-        lax.fori_loop(0, TOK // QB, tokens, 0)
-
-    new_sq = jnp.zeros((1, FWD), F32)
-    for c in range(len(CHUNKS)):
-        ag1_end(c)
-        apply(c, c == 0)
-        base, width, *_ = sizes(c)
-        u = nstack[pl.ds(base + 2 * width, width), :].astype(F32)
-        new_sq = new_sq + jnp.sum(u * u, axis=0, keepdims=True)
-    old = w2_v[...]
-    factor = jnp.sqrt(jnp.sum(old * old, axis=0, keepdims=True)) / jnp.sqrt(new_sq + EPS)
-
-    for h in range(HEADS):
-        o_copy(h).wait_recv()
-    lse_copy().wait_recv()
-    for i in range(TOK // HD):
-        tok = pl.ds(i * HD, HD)
-        theirs = jnp.concatenate([lse_recv[:, tok], jnp.zeros((HD - 8, HD), F32)], axis=0).T
-        theirs = jnp.where(seq == 0, NEG, theirs)
-        keep = 1.0 / (1.0 + jnp.exp2(theirs - lse_own[tok, :]))
-        for h in range(HEADS):
-            k = keep[:, h : h + 1]
-            o = o_own[tok, lanes(h)].astype(F32) * k + o_recv[h, tok, :].astype(F32) * (1.0 - k)
-            out[tok, lanes(h)] = (o + acc[tok, lanes(h)] * factor[:, h * HD : (h + 1) * HD]).astype(BF)
-
-    for h in range(HEADS):
-        q_copy(h).wait_send()
-        o_copy(h).wait_send()
+                for cp in kv_copies(h, b):
+                    cp.wait_send()
     lse_copy().wait_send()
     for c in range(len(CHUNKS)):
         for cp in (*rs1_copies(c), *rs2_copies(c), *ag2_copies(c), *ag1_copies(c)):
@@ -428,7 +504,7 @@
     half = [3 * w // 8 for _, w, _ in CHUNKS]
     share = max(up16(3 * w // 16) for _, w, _ in CHUNKS)
     scratch = [
-        act, act, act, act, act, act, pltpu.VMEM((rows, 1), F32), weight, weight, weight,
+        act, act, act, act, act, act, pltpu.VMEM((1, rows), F32), weight, weight, weight,
         pltpu.VMEM((3 * FWD, FWD), F32),
         pltpu.VMEM((3 * FWD, FWD), BF),
         pltpu.VMEM((3 * FWD, FWD), F32),
@@ -441,24 +517,25 @@
         pltpu.VMEM((n, share, FWD), BF),
         pltpu.VMEM((n, 3, share, FWD), BF),
         pltpu.VMEM((3 * FWD, FWD), BF),
+        pltpu.VMEM((SERVED, rows, HD), BF),
+        pltpu.VMEM((KV_HEADS, rows, HD), BF),
+        pltpu.VMEM((KV_HEADS, rows, HD), BF),
+        pltpu.VMEM((SERVED, rows, HD), BF),
         pltpu.VMEM((HEADS, rows, HD), BF),
-        pltpu.VMEM((HEADS, rows, HD), BF),
-        pltpu.VMEM((HEADS, rows, HD), BF),
-        act,
+        pltpu.VMEM((rows, FWD), F32),
+        pltpu.VMEM((rows, HD), F32),
         pltpu.VMEM((rows, HD), F32),
         pltpu.VMEM((rows, HD), F32),
         pltpu.VMEM((8, rows), F32),
         pltpu.VMEM((8, rows), F32),
         pltpu.VMEM((rows, FWD), F32),
         pltpu.SemaphoreType.DMA((10,)),
-        pltpu.SemaphoreType.DMA((HEADS,)),
-        pltpu.SemaphoreType.DMA((HEADS,)),
-        pltpu.SemaphoreType.DMA((HEADS,)),
-        pltpu.SemaphoreType.DMA((HEADS,)),
+        *[pltpu.SemaphoreType.DMA((SERVED, 2))] * 4,
+        *[pltpu.SemaphoreType.DMA((KV_HEADS, 2, 2))] * 2,
         pltpu.SemaphoreType.DMA((1,)),
         pltpu.SemaphoreType.DMA((1,)),
-        pltpu.SemaphoreType.DMA((n, 16)),
-        pltpu.SemaphoreType.DMA((n, 16)),
+        pltpu.SemaphoreType.DMA((n, 18)),
+        pltpu.SemaphoreType.DMA((n, 18)),
     ]
     square = fast_gate.reshape(FWD, FWD), fast_up.reshape(FWD, FWD), fast_down.reshape(FWD, FWD)
     return pl.pallas_call(
@@ -470,7 +547,7 @@
         compiler_params=pltpu.CompilerParams(
             collective_id=0, has_side_effects=True, vmem_limit_bytes=60 << 20
         ),
-    )(attn_q, attn_k, attn_v, fast_q, fast_k, fast_v, rates, *square)
+    )(attn_q, attn_k, attn_v, fast_q, fast_k, fast_v, rates.reshape(1, rows), *square)
 
 
 def solution(mesh):

time: 104 us -> 81.6 us (0.78)
  the two profiles are of different devices: /device:TPU:72 before, /device:TPU:0 now
where the time goes in v2:
time: 81.6 us; the launch traced here: 81.5 us
  Pallas kernels  79 us (97%)
  local copies, waits for them, and re-layouts  2.49 us (3%)
    pallas_call x1, Pallas kernels, shards(): pl.pallas_call(kernel, out_shape=jax.ShapeDtypeStruct((rows, FWD), BF), i...  79 us
    unnamed x1, local copies, waits for them, and re-layouts  2.49 us

profile of v2, /device:TPU:0, one launch (start us, length us, event | category | flops | bytes accessed | tf_op | source)
XLA Modules:
  0.0 81.5 jit_solution(8109069401065072075)
XLA Ops:
  0.0 79.0 %shard_map.100 = bf16[1024,640]{1,0:T(8,128)(2,1)} custom-call(bf16[1024,640]{1,0:T(8,128)(2,1)} %aq.1, bf16[1024,640]{1,0:T(8,128)(2,1)} %ak.1, bf16[1024,640]{1,0:T(8,128)(2,1)} %av.1, bf16[1024,640]{1,0:T(8,128)(2,1)} %fq.1, bf16[1024,640]{1,0:T(8,128)(2,1)} %fk.1, bf16[1024,640]{1,0:T(8,128)(2,1)} %fv.1, f32[1,1024]{1,0:T(1,128)} %bitcast.7, ...), custom_call_target="tpu_custom_call" | custom-call | tf_op jit(solution)/shard_map/pallas_call | solution.py:541
  79.0 2.5 %copy.12 = bf16[1024,640]{1,0:T(8,128)(2,1)} copy(bf16[1024,640]{1,0:T(8,128)(2,1)} %shard_map.100) | data formatting | bytes 2621440

commit v3 on v2

--- a/solution.py
+++ b/solution.py
@@ -13,6 +13,8 @@
 HEADS = 5
 QB = 256
 TB = 512
+AB = 512
+PIECES = 1
 EPS = 1e-06
 MESH = pl.DeviceIdType.MESH
 SCALE = math.log2(math.e) / math.sqrt(HD)
@@ -44,13 +46,14 @@
 
 
 ORDER = (
-    "q31", "v40", "q30", "G2", "q11", "v41", "o40", "q21", "G1", "G0", "s11", "o00",
-    "m2", "o20", "q20", "q01", "s40", "o30", "o01", "s31", "m0", "m1", "o21", "s30",
-    "e2", "o11", "s41", "e1", "e0", "s01", "q00", "r2", "r1", "r0", "s20", "q10",
-    "a2", "a1", "o10", "o31", "a0", "f2", "f1", "f0", "s21", "o41", "s10", "s00",
-    "P1", "P0", "M", "P2",
+    "q00", "v40", "q31", "q30", "v41", "q20", "G0", "G1", "s31", "q21", "G2", "m0",
+    "m1", "q01", "o41", "s00", "o11", "m2", "o40", "q11", "s30", "o20", "e1", "o01",
+    "e2", "e0", "o30", "s01", "r2", "r1", "r0", "s11", "o21", "q10", "a2", "a1",
+    "s21", "a0", "s40", "o31", "f2", "f1", "s10", "o00", "f0", "s41", "s20", "P2",
+    "o10", "P1", "M", "P0",
 )
 KV_HEADS = 1
+SHIFT = 1
 SERVED = HEADS - KV_HEADS
 
 
@@ -71,7 +74,7 @@
     aq_v, ak_v, av_v, fq_v, fk_v, fv_v, rt_v, w1_v, w3_v, w2_v,
     mstack, mbf, gsum, gbf, rx0, rx1, rx2, fb0, fb1, fb2, part, share_out, share_in,
     new_out, new_in, nstack, qn, kn, vn, o_send, o_recv, o_own, lse_own, lse_nb, lse_kv, lse_send, lse_recv,
-    acc, ld_sem, q_ss, q_rs, o_ss, o_rs, k_ss, k_rs, l_ss, l_rs, c_ss, c_rs,
+    acc, side, res, ld_sem, st_sem, q_ss, q_rs, o_ss, o_rs, k_ss, k_rs, l_ss, l_rs, c_ss, c_rs,
 ):
     seq = lax.axis_index("seq")
     head = lax.axis_index("head")
@@ -91,16 +94,17 @@
     before = (lax.rem(seq + 15, 16), head)
     after = (lax.rem(seq + 1, 16), head)
 
-    loads = []
-    for i, (src, dst) in enumerate(
-        (
-            (w1, w1_v), (w3, w3_v), (w2, w2_v), (fk, fk_v), (fv, fv_v), (rt, rt_v),
-            (ak, ak_v), (av, av_v), (aq, aq_v), (fq, fq_v),
+    loads = [
+        pltpu.make_async_copy(src, dst, ld_sem.at[i])
+        for i, (src, dst) in enumerate(
+            (
+                (fk, fk_v), (w1, w1_v), (w3, w3_v), (w2, w2_v), (fv, fv_v), (rt, rt_v),
+                (aq, aq_v), (ak, ak_v), (av, av_v), (fq, fq_v),
+            )
         )
-    ):
-        c = pltpu.make_async_copy(src, dst, ld_sem.at[i])
+    ]
+    for c in loads[:6]:
         c.start()
-        loads.append(c)
 
     barrier = pltpu.get_barrier_semaphore()
     peers = [at(a, d) for a in ("x", "y") for d in (1, -1, 2)] + [before, after]
@@ -147,18 +151,38 @@
     def rows_of(base, index, n):
         return pl.ds(pl.multiple_of(base + index * n, 8 if n % 16 else 16), n)
 
+    def way(a, k):
+        sign = 1 - 2 * k
+        if a == "x":
+            sign = jnp.where(cy == 0, SHIFT, jnp.where(cy == 3, -SHIFT, sign)) if SHIFT else sign
+        return sign
+
+    def wayg(a, k):
+        return -1 if a == "y" else way(a, k)
+
     def rs1_copies(c):
         base, _, _, p, hf, _, a, _ = sizes(c)
-        up, dn, op = coord(a, 1), coord(a, -1), coord(a, 2)
+        op = coord(a, 2)
         ss, rs, r = c_ss.at[c], c_rs.at[c], rx[c]
-        return (
-            Remote(gbf.at[rows_of(base, op * 2, hf)], r.at[0], ss.at[0], rs.at[0], at(a, 1)),
-            Remote(gbf.at[rows_of(base, op * 2 + 1, hf)], r.at[1], ss.at[1], rs.at[1], at(a, -1)),
-            Remote(gbf.at[rows_of(base, up * 2 + 1, hf)], r.at[2], ss.at[2], rs.at[2], at(a, 1)),
-            Remote(gbf.at[rows_of(base, dn * 2, hf)], r.at[3], ss.at[3], rs.at[3], at(a, -1)),
-            Remote(fb[c].at[0], r.at[4], ss.at[4], rs.at[4], at(a, 1)),
-            Remote(fb[c].at[1], r.at[5], ss.at[5], rs.at[5], at(a, -1)),
-        )
+        copies = []
+        for k in range(2):
+            to = way(a, k)
+            copies.append(
+                Remote(gbf.at[rows_of(base, op * 2 + k, hf)], r.at[k], ss.at[k], rs.at[k], at(a, to))
+            )
+        for k in (1, 0):
+            to = -way(a, k)
+            copies.append(
+                Remote(
+                    gbf.at[rows_of(base, coord(a, to) * 2 + k, hf)], r.at[2 + k],
+                    ss.at[2 + k], rs.at[2 + k], at(a, to),
+                )
+            )
+        for k in range(2):
+            copies.append(
+                Remote(fb[c].at[k], r.at[4 + k], ss.at[4 + k], rs.at[4 + k], at(a, way(a, k)))
+            )
+        return copies
 
     def rs1_start(c):
         for cp in rs1_copies(c)[:4]:
@@ -167,12 +191,11 @@
     def rs1_mid(c):
         base, _, _, _, hf, _, a, _ = sizes(c)
         cps = rs1_copies(c)
-        cps[0].wait_recv()
-        fb[c][0] = (gsum[rows_of(base, coord(a, 1) * 2, hf), :] + rx[c][0].astype(F32)).astype(BF)
-        cps[4].start()
-        cps[1].wait_recv()
-        fb[c][1] = (gsum[rows_of(base, coord(a, -1) * 2 + 1, hf), :] + rx[c][1].astype(F32)).astype(BF)
-        cps[5].start()
+        for k in range(2):
+            cps[k].wait_recv()
+            rows = rows_of(base, coord(a, way(a, k)) * 2 + k, hf)
+            fb[c][k] = (gsum[rows, :] + rx[c][k].astype(F32)).astype(BF)
+            cps[4 + k].start()
 
     def rs2_copies(c):
         _, _, _, _, _, s, _, b = sizes(c)
@@ -193,12 +216,12 @@
             cps[i].wait_recv()
         r = rx[c]
         mine = coord(a)
-        part[pl.ds(0, hf), :] = (
-            gsum[rows_of(base, mine * 2, hf), :] + r[3].astype(F32) + r[4].astype(F32)
-        )
-        part[pl.ds(hf, hf), :] = (
-            gsum[rows_of(base, mine * 2 + 1, hf), :] + r[2].astype(F32) + r[5].astype(F32)
-        )
+        for k in range(2):
+            part[pl.ds(k * hf, hf), :] = (
+                gsum[rows_of(base, mine * 2 + k, hf), :]
+                + r[2 + k].astype(F32)
+                + r[4 + k].astype(F32)
+            )
         for d, cp in zip((1, 2, 3), rs2_copies(c)):
             share_out[c, d - 1, pl.ds(0, s), :] = part[rows_of(0, coord(b, d), s), :].astype(BF)
             cp.start()
@@ -237,18 +260,16 @@
     def ag1_copies(c):
         base, _, _, p, hf, _, a, _ = sizes(c)
         ss, rs = c_ss.at[c], c_rs.at[c]
-        me, dn, up = coord(a), coord(a, -1), coord(a, 1)
-
-        def same(rows, i, d):
-            return Remote(nstack.at[rows], nstack.at[rows], ss.at[i], rs.at[i], at(a, d))
+        me = coord(a)
+
+        def same(index, k, i, to):
+            rows = rows_of(base, index * 2 + k, hf)
+            return Remote(nstack.at[rows], nstack.at[rows], ss.at[i], rs.at[i], at(a, to))
 
         return (
-            same(rows_of(base, me * 2, hf), 12, 1),
-            same(rows_of(base, me * 2 + 1, hf), 13, -1),
-            same(rows_of(base, me * 2 + 1, hf), 16, 1),
-            same(rows_of(base, me * 2, hf), 17, -1),
-            same(rows_of(base, dn * 2, hf), 14, 1),
-            same(rows_of(base, up * 2 + 1, hf), 15, -1),
+            *[same(me, k, 12 + k, wayg(a, k)) for k in range(2)],
+            *[same(me, k, 14 + k, -wayg(a, k)) for k in (1, 0)],
+            *[same(coord(a, -wayg(a, k)), k, 16 + k, wayg(a, k)) for k in range(2)],
         )
 
     def ag2_end(c):
@@ -292,28 +313,30 @@
         base = 3 * first
         rows = [pl.ds(base + n * width, width) for n in range(3)]
 
-        def tokens(i, _):
-            tok = pl.ds(pl.multiple_of(i * TB, TB), TB)
+        for i in range(TOK // TB):
+            tok = pl.ds(i * TB, TB)
             key = fk_v[tok, :]
             val = fv_v[tok, :]
             rate = -rt_v[:, tok]
-            pg = nt(mbf[rows[0], :], key)
-            pu = nt(mbf[rows[1], :], key)
+            pre = nt(mbf[pl.ds(base, 2 * width), :], key)
+            pg, pu = pre[:width], pre[width:]
             hg = nt(mbf[rows[2], :], val) * rate
             sg = jax.nn.sigmoid(pg)
             act = pg * sg
-            hidden = (act * pu * rate).astype(BF)
-            gg = (hg * pu * sg * (1.0 + pg * (1.0 - sg))).astype(BF)
-            ug = (hg * act).astype(BF)
-            for r, lhs, rhs in ((rows[0], gg, key), (rows[1], ug, key), (rows[2], hidden, val)):
-                gsum[r, :] += nn(lhs, rhs)
-            return 0
-
-        for r in rows:
-            gsum[r, :] = jnp.zeros((width, FWD), F32)
-        lax.fori_loop(0, TOK // TB, tokens, 0)
-        whole = pl.ds(base, 3 * width)
-        gbf[whole, :] = gsum[whole, :].astype(BF)
+            side[pl.ds(0, width), :] = (hg * pu * sg * (1.0 + pg * (1.0 - sg))).astype(BF)
+            side[pl.ds(width, width), :] = (hg * act).astype(BF)
+            side[pl.ds(2 * width, width), :] = (act * pu * rate).astype(BF)
+            both = pl.ds(base, 2 * width)
+            in_part = nn(side[pl.ds(0, 2 * width), :], key)
+            out_part = nn(side[pl.ds(2 * width, width), :], val)
+            if i:
+                in_part = gsum[both, :] + in_part
+                out_part = gsum[rows[2], :] + out_part
+            gsum[both, :] = in_part
+            gsum[rows[2], :] = out_part
+            if i == TOK // TB - 1:
+                gbf[both, :] = in_part.astype(BF)
+                gbf[rows[2], :] = out_part.astype(BF)
 
     row_i = lax.broadcasted_iota(jnp.int32, (QB, QB), 0)
     col_i = lax.broadcasted_iota(jnp.int32, (QB, QB), 1)
@@ -396,6 +419,7 @@
                 )
 
     squares = []
+    stores = []
 
     def apply(c, first, last):
         base, width, *_ = sizes(c)
@@ -408,21 +432,31 @@
             )
 
         def tokens(i, _):
-            tok = pl.ds(pl.multiple_of(i * QB, QB), QB)
+            tok = pl.ds(i * AB if last else pl.multiple_of(i * AB, AB), AB)
             q = fq_v[tok, :]
-            pg = nt(q, nstack[pl.ds(base, width), :])
-            pu = nt(q, nstack[pl.ds(base + width, width), :])
+            pre = nt(q, nstack[pl.ds(base, 2 * width), :])
+            pg, pu = pre[:, :width], pre[:, width:]
             hid = (pg * jax.nn.sigmoid(pg) * pu).astype(BF)
             o = nn(hid, nstack[pl.ds(base + 2 * width, width), :])
             if not first:
                 o = acc[tok, :] + o
             if last:
-                out[tok, :] = (o_own[tok, :] + o * factor).astype(BF)
+                res[tok, :] = (o_own[tok, :] + o * factor).astype(BF)
             else:
                 acc[tok, :] = o
             return 0
 
-        lax.fori_loop(0, TOK // QB, tokens, 0)
+        if not last:
+            lax.fori_loop(0, TOK // AB, tokens, 0)
+        else:
+            for i in range(TOK // AB):
+                tokens(i, 0)
+                stores.append(
+                    pltpu.make_async_copy(
+                        res.at[pl.ds(i * AB, AB)], out.at[pl.ds(i * AB, AB)], st_sem.at[i]
+                    )
+                )
+                stores[-1].start()
 
     waited = set()
 
@@ -433,6 +467,7 @@
                 loads[i].wait()
 
     applied = [0]
+    grown = []
     merged = [False]
     left = set((h, b) for h in range(SERVED) for b in range(2))
     for token in ORDER:
@@ -461,6 +496,10 @@
                     send_lse()
         elif kind == "G":
             loaded(*range(6))
+            if not grown:
+                for cp in loads[6:]:
+                    cp.start()
+            grown.append(first)
             prepare(first)
             grads(first)
             rs1_start(first)
@@ -482,6 +521,8 @@
             applied[0] += 1
             apply(first, applied[0] == 1, applied[0] == len(CHUNKS))
 
+    for cp in stores:
+        cp.wait()
     for h in range(HEADS):
         for b in range(2):
             if h < SERVED:
@@ -494,6 +535,10 @@
     for c in range(len(CHUNKS)):
         for cp in (*rs1_copies(c), *rs2_copies(c), *ag2_copies(c), *ag1_copies(c)):
             cp.wait_send()
+
+
+def hand_on(src, dst):
+    dst[...] = src[...]
 
 
 def shards(attn_q, attn_k, attn_v, fast_q, fast_k, fast_v, rates, fast_gate, fast_up, fast_down):
@@ -529,7 +574,10 @@
         pltpu.VMEM((8, rows), F32),
         pltpu.VMEM((8, rows), F32),
         pltpu.VMEM((rows, FWD), F32),
+        pltpu.VMEM((3 * 256, TB), BF),
+        act,
         pltpu.SemaphoreType.DMA((10,)),
+        pltpu.SemaphoreType.DMA((TOK // AB,)),
         *[pltpu.SemaphoreType.DMA((SERVED, 2))] * 4,
         *[pltpu.SemaphoreType.DMA((KV_HEADS, 2, 2))] * 2,
         pltpu.SemaphoreType.DMA((1,)),
@@ -538,16 +586,24 @@
         pltpu.SemaphoreType.DMA((n, 18)),
     ]
     square = fast_gate.reshape(FWD, FWD), fast_up.reshape(FWD, FWD), fast_down.reshape(FWD, FWD)
-    return pl.pallas_call(
+    out = pl.pallas_call(
         kernel,
         out_shape=jax.ShapeDtypeStruct((rows, FWD), BF),
         in_specs=[pl.BlockSpec(memory_space=pl.ANY)] * 10,
-        out_specs=pl.BlockSpec(memory_space=pltpu.VMEM),
+        out_specs=pl.BlockSpec(memory_space=pl.ANY),
         scratch_shapes=scratch,
         compiler_params=pltpu.CompilerParams(
             collective_id=0, has_side_effects=True, vmem_limit_bytes=60 << 20
         ),
     )(attn_q, attn_k, attn_v, fast_q, fast_k, fast_v, rates.reshape(1, rows), *square)
+    block = pl.BlockSpec((rows // PIECES, FWD), lambda i: (i, 0))
+    return pl.pallas_call(
+        hand_on,
+        grid=(PIECES,),
+        out_shape=jax.ShapeDtypeStruct((rows, FWD), BF),
+        in_specs=[block],
+        out_specs=block,
+    )(out)
 
 
 def solution(mesh):

time: 81.6 us -> 75.4 us (0.924)
  Pallas kernels: 79 us -> 74.8 us
  local copies, waits for them, and re-layouts: 2.49 us -> 0 us
    pallas_call x1, Pallas kernels: 79 us -> 72.3 us  [shards(): pl.pallas_call(kernel, out_shape=jax.ShapeDtypeStruct((rows, FWD), BF), i...]
    unnamed x1 -> x0, local copies, waits for them, and re-layouts: 2.49 us -> none
    pallas_call x0 -> x1, Pallas kernels: none -> 2.47 us  [shards(): pl.pallas_call(hand_on, grid=(PIECES,), out_shape=jax.ShapeDtypeStruct((r...]
where the time goes in v3:
time: 75.4 us; the launch traced here: 74.8 us
  Pallas kernels  74.8 us (99%)
    pallas_call x1, Pallas kernels, shards(): pl.pallas_call(kernel, out_shape=jax.ShapeDtypeStruct((rows, FWD), BF), i...  72.3 us
    pallas_call x1, Pallas kernels, shards(): pl.pallas_call(hand_on, grid=(PIECES,), out_shape=jax.ShapeDtypeStruct((r...  2.47 us

profile of v3, /device:TPU:0, one launch (start us, length us, event | category | flops | bytes accessed | tf_op | source)
XLA Modules:
  0.0 74.8 jit_solution(17071641471387400745)
XLA Ops:
  0.0 72.3 %shard_map.100.src = bf16[1024,640]{1,0:T(8,128)(2,1)} custom-call(bf16[1024,640]{1,0:T(8,128)(2,1)} %aq.1, bf16[1024,640]{1,0:T(8,128)(2,1)} %ak.1, bf16[1024,640]{1,0:T(8,128)(2,1)} %av.1, bf16[1024,640]{1,0:T(8,128)(2,1)} %fq.1, bf16[1024,640]{1,0:T(8,128)(2,1)} %fk.1, bf16[1024,640]{1,0:T(8,128)(2,1)} %fv.1, f32[1,1024]{1,0:T(1,128)} %bitcast.7, ...), custom_call_target="tpu_custom_call" | custom-call | tf_op jit(solution)/shard_map/pallas_call | solution.py:589
  72.3 2.5 %shard_map.101 = bf16[1024,640]{1,0:T(8,128)(2,1)} custom-call(bf16[1024,640]{1,0:T(8,128)(2,1)} %shard_map.100.src), custom_call_target="tpu_custom_call" | custom-call | tf_op jit(solution)/shard_map/pallas_call | solution.py:600

commit v4 on v3

--- a/solution.py
+++ b/solution.py
@@ -14,7 +14,7 @@
 QB = 256
 TB = 512
 AB = 512
-PIECES = 1
+PIECES = 2
 EPS = 1e-06
 MESH = pl.DeviceIdType.MESH
 SCALE = math.log2(math.e) / math.sqrt(HD)
@@ -47,9 +47,9 @@
 
 ORDER = (
     "q00", "v40", "q31", "q30", "v41", "q20", "G0", "G1", "s31", "q21", "G2", "m0",
-    "m1", "q01", "o41", "s00", "o11", "m2", "o40", "q11", "s30", "o20", "e1", "o01",
+    "m1", "q01", "o41", "s00", "o11", "m2", "o40", "s30", "o20", "e1", "q11", "o01",
     "e2", "e0", "o30", "s01", "r2", "r1", "r0", "s11", "o21", "q10", "a2", "a1",
-    "s21", "a0", "s40", "o31", "f2", "f1", "s10", "o00", "f0", "s41", "s20", "P2",
+    "s21", "a0", "s20", "s40", "o31", "f2", "f1", "s10", "o00", "f0", "s41", "P2",
     "o10", "P1", "M", "P0",
 )
 KV_HEADS = 1
@@ -94,12 +94,18 @@
     before = (lax.rem(seq + 15, 16), head)
     after = (lax.rem(seq + 1, 16), head)
 
+    early = pl.ds(CHUNKS[0][0], CHUNKS[0][1])
+    late = pl.ds(CHUNKS[0][1], FWD - CHUNKS[0][1])
     loads = [
         pltpu.make_async_copy(src, dst, ld_sem.at[i])
         for i, (src, dst) in enumerate(
             (
-                (fk, fk_v), (w1, w1_v), (w3, w3_v), (w2, w2_v), (fv, fv_v), (rt, rt_v),
+                (fk, fk_v), (w1.at[:, early], w1_v.at[:, early]),
+                (w3.at[:, early], w3_v.at[:, early]), (w2.at[early], w2_v.at[early]),
+                (fv, fv_v), (rt, rt_v),
                 (aq, aq_v), (ak, ak_v), (av, av_v), (fq, fq_v),
+                (w1.at[:, late], w1_v.at[:, late]),
+                (w3.at[:, late], w3_v.at[:, late]), (w2.at[late], w2_v.at[late]),
             )
         )
     ]
@@ -497,8 +503,10 @@
         elif kind == "G":
             loaded(*range(6))
             if not grown:
-                for cp in loads[6:]:
-                    cp.start()
+                for i in (10, 11, 12, 6, 7, 8, 9):
+                    loads[i].start()
+            else:
+                loaded(10, 11, 12)
             grown.append(first)
             prepare(first)
             grads(first)
@@ -576,7 +584,7 @@
         pltpu.VMEM((rows, FWD), F32),
         pltpu.VMEM((3 * 256, TB), BF),
         act,
-        pltpu.SemaphoreType.DMA((10,)),
+        pltpu.SemaphoreType.DMA((13,)),
         pltpu.SemaphoreType.DMA((TOK // AB,)),
         *[pltpu.SemaphoreType.DMA((SERVED, 2))] * 4,
         *[pltpu.SemaphoreType.DMA((KV_HEADS, 2, 2))] * 2,

time: 75.4 us -> 74.6 us (0.989)
  Pallas kernels: 74.8 us -> 74 us
where the time goes in v4:
time: 74.6 us; the launch traced here: 74 us
  Pallas kernels  74 us (99%)
    pallas_call x1, Pallas kernels, shards(): pl.pallas_call(kernel, out_shape=jax.ShapeDtypeStruct((rows, FWD), BF), i...  71.8 us
    pallas_call x1, Pallas kernels, shards(): pl.pallas_call(hand_on, grid=(PIECES,), out_shape=jax.ShapeDtypeStruct((r...  2.2 us

profile of v4, /device:TPU:0, one launch (start us, length us, event | category | flops | bytes accessed | tf_op | source)
XLA Modules:
  0.0 74.0 jit_solution(4196884037678367883)
XLA Ops:
  0.0 71.8 %shard_map.100.src = bf16[1024,640]{1,0:T(8,128)(2,1)} custom-call(bf16[1024,640]{1,0:T(8,128)(2,1)} %aq.1, bf16[1024,640]{1,0:T(8,128)(2,1)} %ak.1, bf16[1024,640]{1,0:T(8,128)(2,1)} %av.1, bf16[1024,640]{1,0:T(8,128)(2,1)} %fq.1, bf16[1024,640]{1,0:T(8,128)(2,1)} %fk.1, bf16[1024,640]{1,0:T(8,128)(2,1)} %fv.1, f32[1,1024]{1,0:T(1,128)} %bitcast.7, ...), custom_call_target="tpu_custom_call" | custom-call | tf_op jit(solution)/shard_map/pallas_call | solution.py:597
  71.8 2.2 %shard_map.101 = bf16[1024,640]{1,0:T(8,128)(2,1)} custom-call(bf16[1024,640]{1,0:T(8,128)(2,1)} %shard_map.100.src), custom_call_target="tpu_custom_call" | custom-call | tf_op jit(solution)/shard_map/pallas_call | solution.py:608
